TPU v7x, 32 devices: a whole 2x2x4 slice. The times are simulated.
32 devices in a mesh: dp: 4 (over y, x), expert: 8 (over z, core).
Axes of the slice: x: 2, y: 2, z: 4, core: 2. Of those that a mesh axis runs over, the one named last changes fastest.
Arguments:
- block_input: bfloat16 [6304, 768], P(('dp', 'expert')), may hold values from -12 to 12
- w_qkv: bfloat16 [768, 2304], P('dp'), may hold values from -0.21875 to 0.21875
- b_q: bfloat16 [768], P('dp'), may hold values from -3 to 3
- b_v: bfloat16 [768], P('dp'), may hold values from -3 to 3
- w_proj: bfloat16 [768, 768], P('dp'), may hold values from -1.75 to 1.75
- b_proj: bfloat16 [768], P('dp'), may hold values from -3 to 3
- ln1_gain: bfloat16 [768], P('dp'), may hold values from 0.099609375 to 1.8984375
- ln1_bias: bfloat16 [768], P('dp'), may hold values from -3 to 3
- ln2_gain: bfloat16 [768], P('dp'), may hold values from 0.099609375 to 1.8984375
- ln2_bias: bfloat16 [768], P('dp'), may hold values from -3 to 3
- w_router: bfloat16 [768, 8], P('dp'), may hold values from -0.4375 to 0.4375
- w_in: bfloat16 [8, 768, 3072], P('expert'), may hold values from -0.21875 to 0.21875
- b_in: bfloat16 [8, 3072], P('expert'), may hold values from -3 to 3
- w_out: bfloat16 [8, 3072, 768], P('expert'), may hold values from -0.109375 to 0.109375
- b_out: bfloat16 [8, 768], P('expert'), may hold values from -3 to 3
- routes: int32 [6304, 2], P(('dp', 'expert')), may hold values from 0 to 7, as said below
- slot_index: int32 [6304, 2], P(('dp', 'expert')), may hold values from 0 to 49, as said below
- d_out: bfloat16 [6304, 768], P(('dp', 'expert')), may hold values from -6 to 6
Outputs:
- block_out: bfloat16 [6304, 768], P(('dp', 'expert'))
- grad_input: float32 [6304, 768], P(('dp', 'expert'))
- d_w_qkv: float32 [768, 2304], P('dp')
- d_b_q: float32 [768], P('dp')
- d_b_v: float32 [768], P('dp')
- d_w_proj: float32 [768, 768], P('dp')
- d_b_proj: float32 [768], P('dp')
- d_ln1_gain: float32 [768], P('dp')
- d_ln1_bias: float32 [768], P('dp')
- d_ln2_gain: float32 [768], P('dp')
- d_ln2_bias: float32 [768], P('dp')
- d_w_router: float32 [768, 8], P('dp')
- d_w_in: float32 [8, 768, 3072], P('expert', 'dp')
- d_b_in: float32 [8, 3072], P('expert', 'dp')
- d_w_out: float32 [8, 3072, 768], P('expert', 'dp')
- d_b_out: float32 [8, 768], P('expert', 'dp')
Inputs may be any that keep to these rules, and one draw needn't show every extreme that they name: `routes`: each token names two different experts. slot_index[t, k] is the arrival position of choice k of token t at expert routes[t, k] among the tokens of one device, all first choices in token order before all second choices; 49 marks a choice that arrives beyond capacity and is dropped. In every draw one expert receives more than 49 first choices from every device.
All inputs are finite; a program needn't handle non-finite values.
Results may differ from a plain program's by a relative error of at most 0.012.
The roundings to bfloat16 on the way count: a program that leaves them out, or rounds other values in their place, can miss the bound.
Values may be sent and summed in bfloat16 or wider, within the bound.
No kernel may reach another device: no remote copies, remote signals or barrier semaphores. Data moves between devices by JAX's collectives and lax.ppermute only.
A program may use at most 128 MiB of HBM per device.

v0:
```python
import math
import jax
import jax.numpy as jnp
from jax import lax
from jax.sharding import PartitionSpec as P

HEAD_DIM = 64
SEQ = 197
NORM_EPS = 1e-06
SQRT_HALF = 0.7071067811865476
INV_ROOT_TWO_PI = 0.3989422804014327


def normalize(values):
    center = values - jnp.mean(values, axis=-1, keepdims=True)
    inv_std = lax.rsqrt(jnp.mean(center * center, axis=-1, keepdims=True) + NORM_EPS)
    return (center * inv_std, inv_std)


def norm_back(grad_in, normed, inv_std, gain_vec):
    scaled = grad_in * gain_vec
    mean_plain = jnp.mean(scaled, axis=-1, keepdims=True)
    mean_mixed = jnp.mean(scaled * normed, axis=-1, keepdims=True)
    return inv_std * (scaled - mean_plain - normed * mean_mixed)


def gelu_value(pre_act):
    return 0.5 * pre_act * (1.0 + lax.erf(pre_act * SQRT_HALF))


def gelu_slope(pre_act):
    return 0.5 * (1.0 + lax.erf(pre_act * SQRT_HALF)) + pre_act * INV_ROOT_TWO_PI * jnp.exp(
        -0.5 * pre_act * pre_act
    )


def by_heads(values, images):
    return values.reshape(images, SEQ, values.shape[1] // HEAD_DIM, HEAD_DIM)


def unpack(full_vectors):
    wide_vectors = full_vectors.astype(jnp.float32)
    return tuple((wide_vectors[index] for index in range(7)))


def slot_tables(routes, slot_table, experts, capacity):
    kept_mask = slot_table < capacity
    target = jnp.where(kept_mask, routes * capacity + slot_table, -1).reshape(-1)
    slot_match = target[:, None] == lax.broadcasted_iota(jnp.int32, (1, experts * capacity), 1)
    filled = jnp.any(slot_match, axis=0)
    choice_ids = lax.broadcasted_iota(jnp.int32, (target.shape[0], 1), 0)
    source = jnp.sum(jnp.where(slot_match, choice_ids, 0), axis=0, dtype=jnp.int32)
    return (kept_mask.reshape(-1), jnp.maximum(target, 0), filled, source)


def per_device(
    block_input,
    w_qkv,
    b_q,
    b_v,
    w_proj,
    b_proj,
    ln1_gain,
    ln1_bias,
    ln2_gain,
    ln2_bias,
    w_router,
    w_in,
    b_in,
    w_out,
    b_out,
    routes,
    slot_index,
    d_out,
):
    tokens = block_input.shape[0]
    width = block_input.shape[1]
    images = tokens // SEQ
    local_count = w_in.shape[0]
    hidden_units = w_in.shape[2]
    experts = local_count * lax.axis_size("expert")
    capacity = 2 * tokens // experts
    score_scale = 1.0 / math.sqrt(HEAD_DIM)
    vectors = jnp.stack([b_q, b_v, b_proj, ln1_gain, ln1_bias, ln2_gain, ln2_bias])
    full_qkv, full_proj, full_router, full_vectors = (
        lax.all_gather(w_qkv, "dp", axis=0, tiled=True),
        lax.all_gather(w_proj, "dp", axis=0, tiled=True),
        lax.all_gather(w_router, "dp", axis=0, tiled=True),
        lax.all_gather(vectors, "dp", axis=1, tiled=True),
    )
    bias_q, bias_v, bias_proj, gain_one, bias_one, gain_two, bias_two = unpack(full_vectors)
    resid = block_input.astype(jnp.float32)
    normed_one, inv_one = normalize(resid)
    a_in = (normed_one * gain_one + bias_one).astype(jnp.bfloat16)
    qkv = jnp.dot(a_in, full_qkv, preferred_element_type=jnp.float32)
    queries = (qkv[:, :width] + bias_q).astype(jnp.bfloat16)
    key_vecs = qkv[:, width : 2 * width].astype(jnp.bfloat16)
    values = (qkv[:, 2 * width :] + bias_v).astype(jnp.bfloat16)
    query_heads = by_heads(queries, images)
    key_heads = by_heads(key_vecs, images)
    value_heads = by_heads(values, images)
    scores = (
        jnp.einsum("bqhd,bkhd->bhqk", query_heads, key_heads, preferred_element_type=jnp.float32)
        * score_scale
    )
    row_max = jnp.max(scores, axis=-1, keepdims=True)
    exp_scores = jnp.exp(scores - row_max)
    row_total = jnp.sum(exp_scores, axis=-1, keepdims=True)
    log_total = row_max + jnp.log(row_total)
    probs_low = (exp_scores / row_total).astype(jnp.bfloat16)
    context = (
        jnp.einsum("bhqk,bkhd->bqhd", probs_low, value_heads, preferred_element_type=jnp.float32)
        .reshape(tokens, width)
        .astype(jnp.bfloat16)
    )
    hidden = resid + jnp.dot(context, full_proj, preferred_element_type=jnp.float32) + bias_proj
    normed_two, inv_two = normalize(hidden)
    y_in = (normed_two * gain_two + bias_two).astype(jnp.bfloat16)
    logits = jnp.dot(y_in, full_router, preferred_element_type=jnp.float32)
    route_hot = (routes[:, :, None] == lax.broadcasted_iota(jnp.int32, (1, 1, experts), 2)).astype(
        jnp.float32
    )
    chosen = jnp.sum(logits[:, None, :] * route_hot, axis=-1)
    first_gate = jax.nn.sigmoid(chosen[:, 0] - chosen[:, 1])
    gate_vals = jnp.stack([first_gate, 1.0 - first_gate], axis=1)
    kept_flat, fetch_index, filled, source = slot_tables(routes, slot_index, experts, capacity)
    sent_slots = jnp.where(filled[:, None], y_in[source // 2], 0).reshape(experts, capacity, width)
    bias_in = b_in.astype(jnp.float32)
    bias_out = b_out.astype(jnp.float32)
    received = lax.all_to_all(sent_slots, "expert", split_axis=0, concat_axis=0, tiled=True)
    slot_count = received.shape[1]
    grouped = received.reshape(-1, local_count, slot_count, width)
    pre_act = (
        jnp.einsum("necd,edf->necf", grouped, w_in, preferred_element_type=jnp.float32)
        + bias_in[None, :, None, :]
    )
    activated = gelu_value(pre_act).astype(jnp.bfloat16)
    down_proj = (
        jnp.einsum("necf,efd->necd", activated, w_out, preferred_element_type=jnp.float32)
        + bias_out[None, :, None, :]
    )
    received, pre_all, act_all, expert_out = (
        received,
        pre_act.reshape(-1, slot_count, hidden_units),
        activated.reshape(-1, slot_count, hidden_units),
        down_proj.astype(jnp.bfloat16).reshape(-1, slot_count, width),
    )
    returned = lax.all_to_all(expert_out, "expert", split_axis=0, concat_axis=0, tiled=True)
    picked = jnp.where(
        kept_flat[:, None],
        returned.reshape(experts * capacity, width)[fetch_index].astype(jnp.float32),
        0.0,
    ).reshape(tokens, 2, width)
    block_out = (hidden + jnp.sum(gate_vals[:, :, None] * picked, axis=1)).astype(jnp.bfloat16)
    grad_out = d_out.astype(jnp.float32)
    d_choice = (
        (gate_vals[:, :, None] * grad_out[:, None, :])
        .reshape(2 * tokens, width)
        .astype(jnp.bfloat16)
    )
    d_sent = jnp.where(filled[:, None], d_choice[source], 0).reshape(experts, capacity, width)
    d_gate = jnp.sum(grad_out[:, None, :] * picked, axis=-1)
    d_diff = (d_gate[:, 0] - d_gate[:, 1]) * gate_vals[:, 0] * gate_vals[:, 1]
    d_logits = (d_diff[:, None] * (route_hot[:, 0] - route_hot[:, 1])).astype(jnp.bfloat16)
    d_received = lax.all_to_all(d_sent, "expert", split_axis=0, concat_axis=0, tiled=True)
    grad_rows = d_received.reshape(-1, local_count, capacity, width)
    act_rows = act_all.reshape(-1, local_count, capacity, hidden_units)
    pre_rows = pre_all.reshape(-1, local_count, capacity, hidden_units)
    recv_rows = received.reshape(-1, local_count, capacity, width)
    d_b_out = jnp.sum(grad_rows.astype(jnp.float32), axis=(0, 2))
    d_w_out = jnp.einsum("necf,necd->efd", act_rows, grad_rows, preferred_element_type=jnp.float32)
    d_pre = jnp.einsum(
        "necd,efd->necf", grad_rows, w_out, preferred_element_type=jnp.float32
    ) * gelu_slope(pre_rows)
    d_b_in = jnp.sum(d_pre, axis=(0, 2))
    d_pre_low = d_pre.astype(jnp.bfloat16)
    d_w_in = jnp.einsum("necd,necf->edf", recv_rows, d_pre_low, preferred_element_type=jnp.float32)
    d_expert_in = (
        jnp.einsum("necf,edf->necd", d_pre_low, w_in, preferred_element_type=jnp.float32)
        .astype(jnp.bfloat16)
        .reshape(-1, capacity, width)
    )
    d_returned = lax.all_to_all(d_expert_in, "expert", split_axis=0, concat_axis=0, tiled=True)
    part_w_in, part_w_out, part_b_in, part_b_out = (
        lax.psum_scatter(d_w_in, "dp", scatter_dimension=1, tiled=True),
        lax.psum_scatter(d_w_out, "dp", scatter_dimension=1, tiled=True),
        lax.psum_scatter(d_b_in, "dp", scatter_dimension=1, tiled=True),
        lax.psum_scatter(d_b_out, "dp", scatter_dimension=1, tiled=True),
    )
    full_qkv, full_proj, full_router, full_vectors = (
        lax.all_gather(w_qkv, "dp", axis=0, tiled=True),
        lax.all_gather(w_proj, "dp", axis=0, tiled=True),
        lax.all_gather(w_router, "dp", axis=0, tiled=True),
        lax.all_gather(vectors, "dp", axis=1, tiled=True),
    )
    bias_q, bias_v, bias_proj, gain_one, bias_one, gain_two, bias_two = unpack(full_vectors)
    back_rows = jnp.where(
        kept_flat[:, None],
        d_returned.reshape(experts * capacity, width)[fetch_index].astype(jnp.float32),
        0.0,
    ).reshape(tokens, 2, width)
    d_w_router = jnp.einsum("td,te->de", y_in, d_logits, preferred_element_type=jnp.float32)
    d_y = jnp.sum(back_rows, axis=1) + jnp.einsum(
        "te,de->td", d_logits, full_router, preferred_element_type=jnp.float32
    )
    d_gain_two = jnp.sum(d_y * normed_two, axis=0)
    d_bias_two = jnp.sum(d_y, axis=0)
    d_hidden = grad_out + norm_back(d_y, normed_two, inv_two, gain_two)
    d_b_proj = jnp.sum(d_hidden, axis=0)
    d_hidden_low = d_hidden.astype(jnp.bfloat16)
    d_w_proj = jnp.einsum("td,te->de", context, d_hidden_low, preferred_element_type=jnp.float32)
    d_context = jnp.einsum(
        "te,de->td", d_hidden_low, full_proj, preferred_element_type=jnp.float32
    ).astype(jnp.bfloat16)
    grad_heads = by_heads(d_context, images)
    probs = jnp.exp(
        jnp.einsum("bqhd,bkhd->bhqk", query_heads, key_heads, preferred_element_type=jnp.float32)
        * score_scale
        - log_total
    )
    d_probs = jnp.einsum(
        "bqhd,bkhd->bhqk", grad_heads, value_heads, preferred_element_type=jnp.float32
    )
    d_values = jnp.einsum(
        "bhqk,bqhd->bkhd",
        probs.astype(jnp.bfloat16),
        grad_heads,
        preferred_element_type=jnp.float32,
    ).reshape(tokens, width)
    row_delta = jnp.sum(probs * d_probs, axis=-1, keepdims=True)
    d_scores = (probs * (d_probs - row_delta) * score_scale).astype(jnp.bfloat16)
    d_queries = jnp.einsum(
        "bhqk,bkhd->bqhd", d_scores, key_heads, preferred_element_type=jnp.float32
    ).reshape(tokens, width)
    d_keys = jnp.einsum(
        "bhqk,bqhd->bkhd", d_scores, query_heads, preferred_element_type=jnp.float32
    ).reshape(tokens, width)
    d_b_q = jnp.sum(d_queries, axis=0)
    d_b_v = jnp.sum(d_values, axis=0)
    d_qkv = jnp.concatenate([d_queries, d_keys, d_values], axis=1).astype(jnp.bfloat16)
    d_w_qkv = jnp.einsum("td,te->de", a_in, d_qkv, preferred_element_type=jnp.float32)
    d_a = jnp.einsum("te,de->td", d_qkv, full_qkv, preferred_element_type=jnp.float32)
    d_gain_one = jnp.sum(d_a * normed_one, axis=0)
    d_bias_one = jnp.sum(d_a, axis=0)
    d_input = d_hidden + norm_back(d_a, normed_one, inv_one, gain_one)
    grad_vectors = jnp.stack(
        [d_b_q, d_b_v, d_b_proj, d_gain_one, d_bias_one, d_gain_two, d_bias_two]
    )
    part_qkv, part_proj, part_router, part_vectors = (
        lax.psum_scatter(d_w_qkv, "dp", scatter_dimension=0, tiled=True),
        lax.psum_scatter(d_w_proj, "dp", scatter_dimension=0, tiled=True),
        lax.psum_scatter(d_w_router, "dp", scatter_dimension=0, tiled=True),
        lax.psum_scatter(grad_vectors, "dp", scatter_dimension=1, tiled=True),
    )
    sum_qkv, sum_proj, sum_router, sum_vectors = lax.psum(
        (part_qkv, part_proj, part_router, part_vectors), "expert"
    )
    return (
        block_out,
        d_input,
        sum_qkv,
        sum_vectors[0],
        sum_vectors[1],
        sum_proj,
        sum_vectors[2],
        sum_vectors[3],
        sum_vectors[4],
        sum_vectors[5],
        sum_vectors[6],
        sum_router,
        part_w_in,
        part_b_in,
        part_w_out,
        part_b_out,
    )


def solution(mesh):
    return jax.shard_map(
        per_device,
        mesh=mesh,
        in_specs=(
            P(("dp", "expert"), None),
            P("dp", None),
            P("dp"),
            P("dp"),
            P("dp", None),
            P("dp"),
            P("dp"),
            P("dp"),
            P("dp"),
            P("dp"),
            P("dp", None),
            P("expert", None, None),
            P("expert", None),
            P("expert", None, None),
            P("expert", None),
            P(("dp", "expert"), None),
            P(("dp", "expert"), None),
            P(("dp", "expert"), None),
        ),
        out_specs=(
            P(("dp", "expert"), None),
            P(("dp", "expert"), None),
            P("dp", None),
            P("dp"),
            P("dp"),
            P("dp", None),
            P("dp"),
            P("dp"),
            P("dp"),
            P("dp"),
            P("dp"),
            P("dp", None),
            P("expert", "dp", None),
            P("expert", "dp"),
            P("expert", "dp", None),
            P("expert", "dp"),
        ),
        check_vma=False,
    )
```

profile of v0, /device:TPU:0, one launch (start us, length us, event | category | flops | bytes accessed | tf_op | source)
XLA Modules:
  0.0 757.3 jit_solution(14147222516695071942)
XLA Ops:
  18.7 9.8 %all-gather = bf16[4,192,7]{1,2,0:T(8,128)(2,1)S(1)} all-gather(bf16[1,192,7]{1,2,0:T(8,128)(2,1)S(1)} %bitcast.203), channel_id=1, replica_groups=mesh['dp'=4,'expert'=8] {'dp'}, dimensions={0}, use_global_device_ids=true | all-gather | bytes 13440 | tf_op jit(solution)/shard_map/all_gather | solution.py:89
  29.9 30.1 %all-gather.5.cloned.1.call-done = bf16[768,2304]{1,0:T(8,128)(2,1)} async-done(((bf16[192,2304]{1,0:T(8,128)(2,1)}), bf16[768,2304]{1,0:T(8,128)(2,1)}) %all-gather.5.cloned.1.call-update) | async-done | bytes 3538960 | tf_op jit(solution)/shard_map/all_gather | solution.py:86
  69.3 20.2 %all-gather.7.cloned.1.call-done = bf16[768,768]{1,0:T(8,128)(2,1)} async-done(((bf16[192,768]{1,0:T(8,128)(2,1)}), bf16[768,768]{1,0:T(8,128)(2,1)}) %all-gather.7.cloned.1.call-update) | async-done | bytes 1179664 | tf_op jit(solution)/shard_map/all_gather | solution.py:87
  103.5 18.8 %all-to-all-done = bf16[8,49,768]{2,1,0:T(8,128)(2,1)S(1)} async-done(((bf16[8,49,768]{2,1,0:T(8,128)(2,1)}), bf16[8,49,768]{2,1,0:T(8,128)(2,1)S(1)}, u32[]{:S(2)}, u32[]{:S(2)}) %all-to-all-start) | async-done | bytes 602144 | tf_op jit(solution)/shard_map/all_to_all | solution.py:130
  122.3 7.4 fusion.12
  129.7 7.1 fusion.44
  141.1 8.6 %all-gather.1 = bf16[4,192,8]{1,2,0:T(8,128)(2,1)S(1)} all-gather(bf16[1,192,8]{1,2,0:T(8,128)(2,1)S(1)} %bitcast.211), channel_id=1, replica_groups=mesh['dp'=4,'expert'=8] {'dp'}, dimensions={0}, use_global_device_ids=true | all-gather | bytes 15360 | tf_op jit(solution)/shard_map/all_gather | solution.py:88
  173.1 21.5 %all_to_all.20 = bf16[8,49,768]{2,1,0:T(8,128)(2,1)S(1)} all-to-all(bf16[8,49,768]{2,1,0:T(8,128)(2,1)S(1)} %broadcast_select_fusion), channel_id=1, replica_groups=mesh['dp'=4,'expert'=8] {'expert'}, dimensions={0} | all-to-all | bytes 1204224 | tf_op jit(solution)/shard_map/all_to_all | solution.py:165
  194.7 7.4 fusion.104
  213.3 16.8 %all-to-all-done.3 = bf16[8,49,768]{2,1,0:T(8,128)(2,1)} async-done(((bf16[8,49,768]{2,1,0:T(8,128)(2,1)}), bf16[8,49,768]{2,1,0:T(8,128)(2,1)}, u32[]{:S(2)}, u32[]{:S(2)}) %all-to-all-start.3) | async-done | bytes 602144 | tf_op jit(solution)/shard_map/all_to_all | solution.py:183
  236.9 7.8 %select_reduce_fusion = (f32[197,768]{1,0:T(8,128)S(1)}, f32[197,768]{1,0:T(8,128)S(1)}) fusion(f32[197,2,768]{2,1,0:T(2,128)} %reshape.385, pred[197,2]{1,0:T(8,128)(4,1)S(1)} %copy-done.27, f32[197,2,768]{2,1,0:T(2,128)} %reshape.384, f32[197,2]{1,0:T(8,128)S(1)} %copy.100), kind=kLoop, calls=%fused_computation.57 | loop fusion | flops 1210368 | bytes 3633074 | tf_op jit(solution)/shard_map/reduce_sum | solution.py:203
  256.8 4.6 fusion.48
  261.5 4.8 fusion.98
  284.6 79.7 %reduce-scatter.17.cloned.1.call-done = f32[192,2304]{1,0:T(8,128)} async-done(((f32[768,2304]{1,0:T(8,128)}), f32[192,2304]{1,0:T(8,128)}) %reduce-scatter.17.cloned.1.call-update) | async-done | bytes 1769488 | tf_op jit(solution)/shard_map/reduce_scatter | solution.py:250
  364.4 6.9 convolution_bitcast_fusion
  372.3 7.0 convolution_bitcast_fusion.1
  379.3 12.0 %reduce-scatter.27.cloned.1.call-done = f32[192,8]{1,0:T(8,128)} async-done(((f32[768,8]{1,0:T(8,128)}), f32[192,8]{1,0:T(8,128)}) %reduce-scatter.27.cloned.1.call-update) | async-done | bytes 6160
  392.3 26.1 %reduce-scatter.31.cloned.1.call-done = f32[192,1]{1,0:T(8,128)} async-done(((f32[768,1]{1,0:T(8,128)}), f32[192,1]{1,0:T(8,128)}) %reduce-scatter.31.cloned.1.call-update) | async-done | bytes 784
  420.0 33.0 %reduce-scatter.29.cloned.1.call-done = f32[768,1]{1,0:T(8,128)} async-done(((f32[3072,1]{1,0:T(8,128)}), f32[768,1]{1,0:T(8,128)}) %reduce-scatter.29.cloned.1.call-update) | async-done | bytes 3088
  455.7 25.0 %reduce-scatter.25.cloned.1.call-done = f32[192,7]{1,0:T(8,128)} async-done(((f32[768,7]{1,0:T(8,128)}), f32[192,7]{1,0:T(8,128)}) %reduce-scatter.25.cloned.1.call-update) | async-done | bytes 5392
  481.7 29.6 %all-reduce = (f32[7,192]{1,0:T(8,128)S(1)}, f32[192,8]{0,1:T(8,128)}) all-reduce(f32[7,192]{1,0:T(8,128)S(1)} %copy.117, f32[192,8]{0,1:T(8,128)S(1)} %copy.119), channel_id=1, replica_groups=mesh['dp'=4,'expert'=8] {'expert'}, use_global_device_ids=true, to_apply=%region_27.28 | all-reduce | flops 2880 | bytes 23040 | tf_op jit(solution)/shard_map/psum | solution.py:255
  511.9 38.5 %all-reduce.4.cloned.1.call-done = (f32[192,2304]{1,0:T(8,128)}, f32[192,768]{1,0:T(8,128)}) async-done(((f32[192,2304]{1,0:T(8,128)}, f32[192,768]{1,0:T(8,128)}), (f32[192,2304]{1,0:T(8,128)}, f32[192,768]{1,0:T(8,128)})) %all-reduce.4.cloned.1.call-update) | async-done | bytes 2359312 | tf_op jit(solution)/shard_map/psum | solution.py:255
  550.4 97.7 %reduce-scatter.23.cloned.1.call-done = f32[1,768,768]{2,1,0:T(8,128)} async-done(((f32[1,3072,768]{2,1,0:T(8,128)}), f32[1,768,768]{2,1,0:T(8,128)}) %reduce-scatter.23.cloned.1.call-update) | async-done | bytes 2359312 | tf_op jit(solution)/shard_map/reduce_scatter | solution.py:186
  648.1 98.8 %reduce-scatter.21.cloned.1.call-done = f32[1,192,3072]{2,1,0:T(8,128)} async-done(((f32[1,768,3072]{2,1,0:T(8,128)}), f32[1,192,3072]{2,1,0:T(8,128)}) %reduce-scatter.21.cloned.1.call-update) | async-done | bytes 2359312 | tf_op jit(solution)/shard_map/reduce_scatter | solution.py:185
  (282 shorter events, 123.2 us)
Async XLA Ops:
  7.2 52.8 %copy-start.2 = (bf16[197,768]{1,0:T(8,128)(2,1)S(1)}, bf16[197,768]{1,0:T(8,128)(2,1)}, u32[]{:S(2)}) copy-start(bf16[197,768]{1,0:T(8,128)(2,1)} %param.18) | copy-start | bytes 907780
  7.2 52.8 %all-gather.5.cloned.1.call-start = ((), (), s32[]{:S(2)}) async-start(), calls=%async_computation.12 | async-start | bytes 4423680 | tf_op jit(solution)/shard_map/all_gather | solution.py:86
  7.9 81.6 %all-gather.7.cloned.1.call-start = ((), (), s32[]{:S(2)}) async-start(), calls=%async_computation.13 | async-start | bytes 1474560 | tf_op jit(solution)/shard_map/all_gather | solution.py:87
  11.7 51.3 %copy-start.42 = (f32[197]{0:T(256)}, f32[197]{0:T(256)S(1)}, u32[]{:S(2)}) copy-start(f32[197]{0:T(256)S(1)} %broadcast_multiply_fusion.5) | copy-start | bytes 2368
  12.9 50.0 %copy-start.46 = (f32[197]{0:T(256)}, f32[197]{0:T(256)S(1)}, u32[]{:S(2)}) copy-start(f32[197]{0:T(256)S(1)} %add_rsqrt_fusion.1) | copy-start | bytes 2368
  29.9 33.1 %copy-start.28 = (f32[768]{0:T(1024)}, f32[768]{0:T(1024)S(1)}, u32[]{:S(2)}) copy-start(f32[768]{0:T(1024)S(1)} %get-tuple-element.32) | copy-start | bytes 9220
  29.9 33.1 %copy-start.30 = (f32[768]{0:T(1024)}, f32[768]{0:T(1024)S(1)}, u32[]{:S(2)}) copy-start(f32[768]{0:T(1024)S(1)} %get-tuple-element.31) | copy-start | bytes 9220
  29.9 61.9 %copy-start.36 = (f32[768]{0:T(1024)}, f32[768]{0:T(1024)S(1)}, u32[]{:S(2)}) copy-start(f32[768]{0:T(1024)S(1)} %get-tuple-element.26) | copy-start | bytes 9220
  98.9 23.5 %all-to-all-start = ((bf16[8,49,768]{2,1,0:T(8,128)(2,1)}), bf16[8,49,768]{2,1,0:T(8,128)(2,1)S(1)}, u32[]{:S(2)}, u32[]{:S(2)}) async-start(bf16[8,49,768]{2,1,0:T(8,128)(2,1)} %broadcast_select_fusion.1), calls=%async_computation | async-start | bytes 1376256 | tf_op jit(solution)/shard_map/all_to_all | solution.py:130
  136.8 23.1 %all-to-all-start.1 = ((bf16[8,49,768]{2,1,0:T(8,128)(2,1)}), bf16[8,49,768]{2,1,0:T(8,128)(2,1)}, u32[]{:S(2)}, u32[]{:S(2)}) async-start(bf16[8,49,768]{2,1,0:T(8,128)(2,1)} %fusion.44), calls=%async_computation.1 | async-start | bytes 1376256 | tf_op jit(solution)/shard_map/all_to_all | solution.py:148
  206.9 23.2 %all-to-all-start.3 = ((bf16[8,49,768]{2,1,0:T(8,128)(2,1)}), bf16[8,49,768]{2,1,0:T(8,128)(2,1)}, u32[]{:S(2)}, u32[]{:S(2)}) async-start(bf16[8,49,768]{2,1,0:T(8,128)(2,1)} %fusion.36), calls=%async_computation.3 | async-start | bytes 1376256 | tf_op jit(solution)/shard_map/all_to_all | solution.py:183
  211.2 73.3 %reduce-scatter.19.cloned.1.call-start = ((), (), s32[]{:S(2)}) async-start(), calls=%async_computation.15 | async-start | bytes 2949120 | tf_op jit(solution)/shard_map/reduce_scatter | solution.py:251
  213.3 31.5 %copy-start.40 = (bf16[197,8]{0,1:T(8,128)(2,1)}, bf16[197,8]{0,1:T(8,128)(2,1)S(1)}, u32[]{:S(2)}) copy-start(bf16[197,8]{0,1:T(8,128)(2,1)S(1)} %fusion.79) | copy-start | bytes 9460
  249.1 115.2 %reduce-scatter.17.cloned.1.call-start = ((), (), s32[]{:S(2)}) async-start(), calls=%async_computation.14 | async-start | bytes 8847360 | tf_op jit(solution)/shard_map/reduce_scatter | solution.py:250
  272.1 119.3 %reduce-scatter.27.cloned.1.call-start = ((), (), s32[]{:S(2)}) async-start(), calls=%async_computation.19 | async-start | bytes 491520
  273.8 144.6 %reduce-scatter.31.cloned.1.call-start = ((), (), s32[]{:S(2)}) async-start(), calls=%async_computation.21 | async-start | bytes 491520
  275.0 178.0 %reduce-scatter.29.cloned.1.call-start = ((), (), s32[]{:S(2)}) async-start(), calls=%async_computation.20 | async-start | bytes 1966080
  276.7 204.0 %reduce-scatter.25.cloned.1.call-start = ((), (), s32[]{:S(2)}) async-start(), calls=%async_computation.18 | async-start | bytes 491520
  280.3 84.0 %copy-start.60 = (f32[1,3072]{1,0:T(1,128)S(1)}, f32[1,3072]{1,0:T(1,128)}, u32[]{:S(2)}) copy-start(f32[1,3072]{1,0:T(1,128)} %copy-done.58) | copy-start | bytes 36868
  281.5 268.9 %all-reduce.4.cloned.1.call-start = ((), (), s32[]{:S(2)}) async-start(), calls=%async_computation.22 | async-start | bytes 4718592 | tf_op jit(solution)/shard_map/psum | solution.py:255
  364.3 283.8 %reduce-scatter.23.cloned.1.call-start = ((), (), s32[]{:S(2)}) async-start(), calls=%async_computation.17 | async-start | bytes 11796480 | tf_op jit(solution)/shard_map/reduce_scatter | solution.py:186
  371.3 375.6 %reduce-scatter.21.cloned.1.call-start = ((), (), s32[]{:S(2)}) async-start(), calls=%async_computation.16 | async-start | bytes 11796480 | tf_op jit(solution)/shard_map/reduce_scatter | solution.py:185
  379.3 75.4 %copy-start.6 = (f32[197,768]{1,0:T(8,128)S(1)}, f32[197,768]{1,0:T(8,128)}, u32[]{:S(2)}) copy-start(f32[197,768]{1,0:T(8,128)} %copy-done.4) | copy-start | bytes 1815556
  550.4 199.3 %copy-start.21 = (f32[192,768]{1,0:T(8,128)S(1)}, f32[192,768]{1,0:T(8,128)}, u32[]{:S(2)}) copy-start(f32[192,768]{1,0:T(8,128)} %get-tuple-element.80) | copy-start | bytes 1769476
  (61 other events, 476.9 us)
Sparse Core Ops, SparseCore 0:
  9.9 50.0 all-gather.4
  61.8 27.7 all-gather.6
  249.2 35.2 reduce-scatter.18
  287.5 76.7 reduce-scatter.16
  366.9 24.3 reduce-scatter.26
  394.0 24.4 reduce-scatter.30
  422.0 30.8 reduce-scatter.28
  456.3 24.4 reduce-scatter.24
  483.2 67.1 all-reduce.3
  554.0 94.1 reduce-scatter.22
  651.8 95.0 reduce-scatter.20
where the time goes:
time: 766 us; the launch traced here: 757 us
  waiting for transfers between devices  506 us (66%)
  matrix products  72.9 us (10%)
  blocking collectives  69.5 us (9%)
  local copies, waits for them, and re-layouts  57.3 us (7%)
  other arithmetic  22.9 us (3%)
  between operations  15 us (2%)
  starting transfers between devices  14 us (2%)
    reduce_scatter x1, waiting for transfers between devices, per_device(): lax.psum_scatter(d_w_in, 'dp', scatter_dimension=1, tiled=True)  98.8 us
    reduce_scatter x1, waiting for transfers between devices, per_device(): lax.psum_scatter(d_w_out, 'dp', scatter_dimension=1, tiled=True)  97.7 us
    unnamed x15, waiting for transfers between devices  97.6 us
    reduce_scatter x1, waiting for transfers between devices, per_device(): lax.psum_scatter(d_w_qkv, 'dp', scatter_dimension=0, tiled=True)  79.7 us
    psum x1, waiting for transfers between devices, per_device(): lax.psum((part_qkv, part_proj, part_router, part_vectors), 'expert')  38.5 us
    all_gather x1, waiting for transfers between devices, per_device(): lax.all_gather(w_qkv, 'dp', axis=0, tiled=True)  30.1 us
    psum x1, blocking collectives, per_device(): lax.psum((part_qkv, part_proj, part_router, part_vectors), 'expert')  29.6 us
    all_to_all x1, blocking collectives, per_device(): lax.all_to_all(d_sent, 'expert', split_axis=0, concat_axis=0, tiled=True)  21.5 us
  transfers between devices with their start and end apart: 14, of which 14 were waited for; matrix products, arithmetic and copies ran while one was open for 10% of the time, Pallas kernels for 0%

commit v1 on v0

--- a/solution.py
+++ b/solution.py
@@ -9,6 +9,19 @@
 NORM_EPS = 1e-06
 SQRT_HALF = 0.7071067811865476
 INV_ROOT_TWO_PI = 0.3989422804014327
+
+
+def ring_gather(shard, axis, dim):
+    ways = lax.axis_size(axis)
+    up = [(d, (d + 1) % ways) for d in range(ways)]
+    down = [(d, (d - 1) % ways) for d in range(ways)]
+    earlier, later = ([shard], [shard])
+    for _ in range(ways // 2):
+        earlier.append(lax.ppermute(earlier[-1], axis, up))
+    for _ in range((ways - 1) // 2):
+        later.append(lax.ppermute(later[-1], axis, down))
+    line = jnp.concatenate([*earlier[::-1], *later[1:]], axis=dim)
+    return jnp.roll(line, (lax.axis_index(axis) - ways // 2) * shard.shape[dim], axis=dim)
 
 
 def normalize(values):
@@ -83,7 +96,7 @@
     score_scale = 1.0 / math.sqrt(HEAD_DIM)
     vectors = jnp.stack([b_q, b_v, b_proj, ln1_gain, ln1_bias, ln2_gain, ln2_bias])
     full_qkv, full_proj, full_router, full_vectors = (
-        lax.all_gather(w_qkv, "dp", axis=0, tiled=True),
+        ring_gather(w_qkv, "dp", 0),
         lax.all_gather(w_proj, "dp", axis=0, tiled=True),
         lax.all_gather(w_router, "dp", axis=0, tiled=True),
         lax.all_gather(vectors, "dp", axis=1, tiled=True),

time: 766 us -> 777 us (1.014)
  waiting for transfers between devices: 506 us -> 489 us
  blocking collectives: 69.5 us -> 82.8 us
  starting transfers between devices: 14 us -> 24.8 us
    all_gather x1, blocking collectives: 9.76 us -> 45.2 us  [per_device(): lax.all_gather(vectors, 'dp', axis=1, tiled=True)]
    all_gather x1, waiting for transfers between devices: 30.1 us -> 0.02 us  [per_device(): lax.all_gather(w_qkv, 'dp', axis=0, tiled=True)]
    all_to_all x1 -> x0, blocking collectives: 21.5 us -> none  [per_device(): lax.all_to_all(d_sent, 'expert', split_axis=0, concat_axis=0, tiled=True)]
    all_gather x1, waiting for transfers between devices: 20.2 us -> 0.01 us  [per_device(): lax.all_gather(w_proj, 'dp', axis=0, tiled=True)]
    all_to_all x0 -> x1, waiting for transfers between devices: none -> 18 us  [per_device(): lax.all_to_all(d_sent, 'expert', split_axis=0, concat_axis=0, tiled=True)]
    ppermute x0 -> x3, waiting for transfers between devices: none -> 15.3 us  [the longest x2 15.3 us: ring_gather(): earlier.append(lax.ppermute(earlier[-1], axis, up))]
    unnamed x154 -> x157, local copies, waits for them, and re-layouts: 19.4 us -> 21.5 us
  transfers between devices with their start and end apart: 14 -> 18, of which waited for: 14 -> 14; matrix products, arithmetic and copies ran while one was open for 10% -> 14% of each run, Pallas kernels for 0% -> 0%
where the time goes in v1:
time: 777 us; the launch traced here: 767 us
  waiting for transfers between devices  489 us (63%)
  blocking collectives  82.8 us (11%)
  matrix products  75 us (10%)
  local copies, waits for them, and re-layouts  57.8 us (7%)
  starting transfers between devices  24.8 us (3%)
  other arithmetic  23.2 us (3%)
  between operations  15.1 us (2%)
    reduce_scatter x1, waiting for transfers between devices, per_device(): lax.psum_scatter(d_w_out, 'dp', scatter_dimension=1, tiled=True)  98.8 us
    reduce_scatter x1, waiting for transfers between devices, per_device(): lax.psum_scatter(d_w_in, 'dp', scatter_dimension=1, tiled=True)  97.7 us
    unnamed x15, waiting for transfers between devices  97.4 us
    reduce_scatter x1, waiting for transfers between devices, per_device(): lax.psum_scatter(d_w_qkv, 'dp', scatter_dimension=0, tiled=True)  79.7 us
    all_gather x1, blocking collectives, per_device(): lax.all_gather(vectors, 'dp', axis=1, tiled=True)  45.2 us
    psum x1, waiting for transfers between devices, per_device(): lax.psum((part_qkv, part_proj, part_router, part_vectors), 'expert')  38.5 us
    psum x1, blocking collectives, per_device(): lax.psum((part_qkv, part_proj, part_router, part_vectors), 'expert')  29.6 us
    unnamed x157, local copies, waits for them, and re-layouts  21.5 us
  transfers between devices with their start and end apart: 18, of which 14 were waited for; matrix products, arithmetic and copies ran while one was open for 14% of the time, Pallas kernels for 0%

profile of v1, /device:TPU:0, one launch (start us, length us, event | category | flops | bytes accessed | tf_op | source)
XLA Modules:
  0.0 767.3 jit_solution(8529553946480580131)
XLA Ops:
  15.9 45.2 %all-gather = bf16[4,192,7]{1,2,0:T(8,128)(2,1)S(1)} all-gather(bf16[1,192,7]{1,2,0:T(8,128)(2,1)S(1)} %bitcast.200), channel_id=1, replica_groups=mesh['dp'=4,'expert'=8] {'dp'}, dimensions={0}, use_global_device_ids=true | all-gather | bytes 13440 | tf_op jit(solution)/shard_map/all_gather | solution.py:102
  69.8 15.3 %collective-permute-done.1 = bf16[192,2304]{1,0:T(8,128)(2,1)S(1)} collective-permute-done((bf16[192,2304]{1,0:T(8,128)(2,1)S(1)}, bf16[192,2304]{1,0:T(8,128)(2,1)S(1)}, u32[]{:S(2)}, u32[]{:S(2)}) %collective-permute-start.1) | collective-permute-done | bytes 884768 | tf_op jit(solution)/shard_map/ppermute | solution.py:20
  103.6 4.9 all-to-all-start
  108.5 18.8 %all-to-all-done = bf16[8,49,768]{2,1,0:T(8,128)(2,1)S(1)} async-done(((bf16[8,49,768]{2,1,0:T(8,128)(2,1)}), bf16[8,49,768]{2,1,0:T(8,128)(2,1)S(1)}, u32[]{:S(2)}, u32[]{:S(2)}) %all-to-all-start) | async-done | bytes 602144 | tf_op jit(solution)/shard_map/all_to_all | solution.py:143
  127.3 7.3 fusion.12
  134.6 7.1 fusion.46
  151.9 7.9 %all-gather.1 = bf16[4,192,8]{1,2,0:T(8,128)(2,1)S(1)} all-gather(bf16[1,192,8]{1,2,0:T(8,128)(2,1)S(1)} %bitcast.208), channel_id=1, replica_groups=mesh['dp'=4,'expert'=8] {'dp'}, dimensions={0}, use_global_device_ids=true | all-gather | bytes 15360 | tf_op jit(solution)/shard_map/all_gather | solution.py:101
  160.6 4.8 all-to-all-done.1
  183.7 18.0 %all-to-all-done.2 = bf16[8,49,768]{2,1,0:T(8,128)(2,1)S(1)} async-done(((bf16[8,49,768]{2,1,0:T(8,128)(2,1)}), bf16[8,49,768]{2,1,0:T(8,128)(2,1)S(1)}, u32[]{:S(2)}, u32[]{:S(2)}) %all-to-all-start.2) | async-done | bytes 602144 | tf_op jit(solution)/shard_map/all_to_all | solution.py:178
  201.8 7.4 fusion.106
  210.8 6.3 fusion.38
  223.4 16.8 %all-to-all-done.3 = bf16[8,49,768]{2,1,0:T(8,128)(2,1)} async-done(((bf16[8,49,768]{2,1,0:T(8,128)(2,1)}), bf16[8,49,768]{2,1,0:T(8,128)(2,1)}, u32[]{:S(2)}, u32[]{:S(2)}) %all-to-all-start.3) | async-done | bytes 602144 | tf_op jit(solution)/shard_map/all_to_all | solution.py:196
  247.1 7.8 %select_reduce_fusion = (f32[197,768]{1,0:T(8,128)S(1)}, f32[197,768]{1,0:T(8,128)S(1)}) fusion(f32[197,2,768]{2,1,0:T(2,128)} %reshape.385, pred[197,2]{1,0:T(8,128)(4,1)S(1)} %copy-done.29, f32[197,2,768]{2,1,0:T(2,128)} %reshape.384, f32[197,2]{1,0:T(8,128)S(1)} %copy.100), kind=kLoop, calls=%fused_computation.59 | loop fusion | flops 1210368 | bytes 3633074 | tf_op jit(solution)/shard_map/reduce_sum | solution.py:216
  294.6 79.7 %reduce-scatter.17.cloned.1.call-done = f32[192,2304]{1,0:T(8,128)} async-done(((f32[768,2304]{1,0:T(8,128)}), f32[192,2304]{1,0:T(8,128)}) %reduce-scatter.17.cloned.1.call-update) | async-done | bytes 1769488 | tf_op jit(solution)/shard_map/reduce_scatter | solution.py:263
  374.3 6.8 convolution_bitcast_fusion.1
  381.9 7.0 convolution_bitcast_fusion
  388.9 12.5 %reduce-scatter.27.cloned.1.call-done = f32[192,8]{1,0:T(8,128)} async-done(((f32[768,8]{1,0:T(8,128)}), f32[192,8]{1,0:T(8,128)}) %reduce-scatter.27.cloned.1.call-update) | async-done | bytes 6160
  402.3 26.1 %reduce-scatter.31.cloned.1.call-done = f32[192,1]{1,0:T(8,128)} async-done(((f32[768,1]{1,0:T(8,128)}), f32[192,1]{1,0:T(8,128)}) %reduce-scatter.31.cloned.1.call-update) | async-done | bytes 784
  430.0 33.0 %reduce-scatter.29.cloned.1.call-done = f32[768,1]{1,0:T(8,128)} async-done(((f32[3072,1]{1,0:T(8,128)}), f32[768,1]{1,0:T(8,128)}) %reduce-scatter.29.cloned.1.call-update) | async-done | bytes 3088
  465.8 25.0 %reduce-scatter.25.cloned.1.call-done = f32[192,7]{1,0:T(8,128)} async-done(((f32[768,7]{1,0:T(8,128)}), f32[192,7]{1,0:T(8,128)}) %reduce-scatter.25.cloned.1.call-update) | async-done | bytes 5392
  491.8 29.6 %all-reduce = (f32[7,192]{1,0:T(8,128)S(1)}, f32[192,8]{0,1:T(8,128)}) all-reduce(f32[7,192]{1,0:T(8,128)S(1)} %copy.117, f32[192,8]{0,1:T(8,128)S(1)} %copy.119), channel_id=1, replica_groups=mesh['dp'=4,'expert'=8] {'expert'}, use_global_device_ids=true, to_apply=%region_27.28 | all-reduce | flops 2880 | bytes 23040 | tf_op jit(solution)/shard_map/psum | solution.py:268
  521.9 38.5 %all-reduce.4.cloned.1.call-done = (f32[192,2304]{1,0:T(8,128)}, f32[192,768]{1,0:T(8,128)}) async-done(((f32[192,2304]{1,0:T(8,128)}, f32[192,768]{1,0:T(8,128)}), (f32[192,2304]{1,0:T(8,128)}, f32[192,768]{1,0:T(8,128)})) %all-reduce.4.cloned.1.call-update) | async-done | bytes 2359312 | tf_op jit(solution)/shard_map/psum | solution.py:268
  560.5 97.7 %reduce-scatter.21.cloned.1.call-done = f32[1,192,3072]{2,1,0:T(8,128)} async-done(((f32[1,768,3072]{2,1,0:T(8,128)}), f32[1,192,3072]{2,1,0:T(8,128)}) %reduce-scatter.21.cloned.1.call-update) | async-done | bytes 2359312 | tf_op jit(solution)/shard_map/reduce_scatter | solution.py:198
  658.2 98.8 %reduce-scatter.23.cloned.1.call-done = f32[1,768,768]{2,1,0:T(8,128)} async-done(((f32[1,3072,768]{2,1,0:T(8,128)}), f32[1,768,768]{2,1,0:T(8,128)}) %reduce-scatter.23.cloned.1.call-update) | async-done | bytes 2359312 | tf_op jit(solution)/shard_map/reduce_scatter | solution.py:199
  (292 shorter events, 129.9 us)
Async XLA Ops:
  7.2 78.1 %copy-start.7 = (bf16[192,2304]{1,0:T(8,128)(2,1)S(1)}, bf16[192,2304]{1,0:T(8,128)(2,1)}, u32[]{:S(2)}) copy-start(bf16[192,2304]{1,0:T(8,128)(2,1)} %param.19) | copy-start | bytes 2654212
  7.2 87.1 %all-gather.5.cloned.1.call-start = ((), (), s32[]{:S(2)}) async-start(), calls=%async_computation.12 | async-start | bytes 1474560 | tf_op jit(solution)/shard_map/all_gather | solution.py:100
  7.2 56.6 %collective-permute-start = (bf16[192,2304]{1,0:T(8,128)(2,1)}, bf16[192,2304]{1,0:T(8,128)(2,1)S(1)}, u32[]{:S(2)}, u32[]{:S(2)}) collective-permute-start(bf16[192,2304]{1,0:T(8,128)(2,1)} %param.19), channel_id=1, source_target_pairs={{0,8},{8,16},{16,24},{24,0},{1,9},{9,17},{17,25},{25,1},{2,10},{10... | collective-permute-start | bytes 2654216 | tf_op jit(solution)/shard_map/ppermute | solution.py:20
  10.2 75.1 %collective-permute-start.2 = (bf16[192,2304]{1,0:T(8,128)(2,1)}, bf16[192,2304]{1,0:T(8,128)(2,1)S(1)}, u32[]{:S(2)}, u32[]{:S(2)}) collective-permute-start(bf16[192,2304]{1,0:T(8,128)(2,1)} %param.19), channel_id=1, source_target_pairs={{0,24},{8,0},{16,8},{24,16},{1,25},{9,1},{17,9},{25,17},{2,26},{10... | collective-permute-start | bytes 2654216 | tf_op jit(solution)/shard_map/ppermute | solution.py:22
  63.9 21.2 %collective-permute-start.1 = (bf16[192,2304]{1,0:T(8,128)(2,1)S(1)}, bf16[192,2304]{1,0:T(8,128)(2,1)S(1)}, u32[]{:S(2)}, u32[]{:S(2)}) collective-permute-start(bf16[192,2304]{1,0:T(8,128)(2,1)S(1)} %collective-permute-done), channel_id=1, source_target_pairs={{0,8},{8,16},{16,24},{24,0},{1,9},{9,17},{17,25},{25,1},{2,10},{10... | collective-permute-start | bytes 2654216 | tf_op jit(solution)/shard_map/ppermute | solution.py:20
  67.5 29.0 %copy-start.38 = (f32[768]{0:T(1024)}, f32[768]{0:T(1024)S(1)}, u32[]{:S(2)}) copy-start(f32[768]{0:T(1024)S(1)} %get-tuple-element.26) | copy-start | bytes 9220
  103.6 23.7 %all-to-all-start = ((bf16[8,49,768]{2,1,0:T(8,128)(2,1)}), bf16[8,49,768]{2,1,0:T(8,128)(2,1)S(1)}, u32[]{:S(2)}, u32[]{:S(2)}) async-start(bf16[8,49,768]{2,1,0:T(8,128)(2,1)} %broadcast_select_fusion.1), calls=%async_computation | async-start | bytes 1376256 | tf_op jit(solution)/shard_map/all_to_all | solution.py:143
  141.7 23.7 %all-to-all-start.1 = ((bf16[8,49,768]{2,1,0:T(8,128)(2,1)}), bf16[8,49,768]{2,1,0:T(8,128)(2,1)}, u32[]{:S(2)}, u32[]{:S(2)}) async-start(bf16[8,49,768]{2,1,0:T(8,128)(2,1)} %fusion.46), calls=%async_computation.1 | async-start | bytes 1376256 | tf_op jit(solution)/shard_map/all_to_all | solution.py:161
  179.4 22.3 %all-to-all-start.2 = ((bf16[8,49,768]{2,1,0:T(8,128)(2,1)}), bf16[8,49,768]{2,1,0:T(8,128)(2,1)S(1)}, u32[]{:S(2)}, u32[]{:S(2)}) async-start(bf16[8,49,768]{2,1,0:T(8,128)(2,1)} %broadcast_select_fusion), calls=%async_computation.2 | async-start | bytes 1376256 | tf_op jit(solution)/shard_map/all_to_all | solution.py:178
  183.0 104.0 %all-gather.7.cloned.1.call-start = ((), (), s32[]{:S(2)}) async-start(), calls=%async_computation.13 | async-start | bytes 4423680 | tf_op jit(solution)/shard_map/all_gather | solution.py:204
  217.0 23.2 %all-to-all-start.3 = ((bf16[8,49,768]{2,1,0:T(8,128)(2,1)}), bf16[8,49,768]{2,1,0:T(8,128)(2,1)}, u32[]{:S(2)}, u32[]{:S(2)}) async-start(bf16[8,49,768]{2,1,0:T(8,128)(2,1)} %fusion.38), calls=%async_computation.3 | async-start | bytes 1376256 | tf_op jit(solution)/shard_map/all_to_all | solution.py:196
  221.4 73.2 %reduce-scatter.19.cloned.1.call-start = ((), (), s32[]{:S(2)}) async-start(), calls=%async_computation.15 | async-start | bytes 2949120 | tf_op jit(solution)/shard_map/reduce_scatter | solution.py:264
  223.4 31.5 %copy-start.42 = (bf16[197,8]{0,1:T(8,128)(2,1)}, bf16[197,8]{0,1:T(8,128)(2,1)S(1)}, u32[]{:S(2)}) copy-start(bf16[197,8]{0,1:T(8,128)(2,1)S(1)} %fusion.81) | copy-start | bytes 9460
  259.3 114.9 %reduce-scatter.17.cloned.1.call-start = ((), (), s32[]{:S(2)}) async-start(), calls=%async_computation.14 | async-start | bytes 8847360 | tf_op jit(solution)/shard_map/reduce_scatter | solution.py:263
  282.3 119.1 %reduce-scatter.27.cloned.1.call-start = ((), (), s32[]{:S(2)}) async-start(), calls=%async_computation.19 | async-start | bytes 491520
  284.0 144.4 %reduce-scatter.31.cloned.1.call-start = ((), (), s32[]{:S(2)}) async-start(), calls=%async_computation.21 | async-start | bytes 491520
  285.2 177.8 %reduce-scatter.29.cloned.1.call-start = ((), (), s32[]{:S(2)}) async-start(), calls=%async_computation.20 | async-start | bytes 1966080
  286.9 203.8 %reduce-scatter.25.cloned.1.call-start = ((), (), s32[]{:S(2)}) async-start(), calls=%async_computation.18 | async-start | bytes 491520
  290.6 83.7 %copy-start.9 = (bf16[8,49,768]{2,1,0:T(8,128)(2,1)S(1)}, bf16[8,49,768]{2,1,0:T(8,128)(2,1)}, u32[]{:S(2)}) copy-start(bf16[8,49,768]{2,1,0:T(8,128)(2,1)} %copy-done.8) | copy-start | bytes 1806340
  291.8 268.6 %all-reduce.4.cloned.1.call-start = ((), (), s32[]{:S(2)}) async-start(), calls=%async_computation.22 | async-start | bytes 4718592 | tf_op jit(solution)/shard_map/psum | solution.py:268
  374.3 283.9 %reduce-scatter.21.cloned.1.call-start = ((), (), s32[]{:S(2)}) async-start(), calls=%async_computation.16 | async-start | bytes 11796480 | tf_op jit(solution)/shard_map/reduce_scatter | solution.py:198
  381.2 375.7 %reduce-scatter.23.cloned.1.call-start = ((), (), s32[]{:S(2)}) async-start(), calls=%async_computation.17 | async-start | bytes 11796480 | tf_op jit(solution)/shard_map/reduce_scatter | solution.py:199
  388.9 75.8 %copy-start.6 = (f32[197,768]{1,0:T(8,128)S(1)}, f32[197,768]{1,0:T(8,128)}, u32[]{:S(2)}) copy-start(f32[197,768]{1,0:T(8,128)} %copy-done.4) | copy-start | bytes 1815556
  560.5 199.3 %copy-start.23 = (f32[192,768]{1,0:T(8,128)S(1)}, f32[192,768]{1,0:T(8,128)}, u32[]{:S(2)}) copy-start(f32[192,768]{1,0:T(8,128)} %get-tuple-element.80) | copy-start | bytes 1769476
  (63 other events, 408.3 us)
Sparse Core Ops, SparseCore 0:
  11.4 42.9 all-gather.4
  185.7 47.4 all-gather.6
  259.4 35.0 reduce-scatter.18
  297.5 76.7 reduce-scatter.16
  376.9 24.4 reduce-scatter.26
  404.0 24.4 reduce-scatter.30
  432.0 30.9 reduce-scatter.28
  466.3 24.4 reduce-scatter.24
  493.2 67.1 all-reduce.3
  564.0 94.1 reduce-scatter.20
  661.9 95.0 reduce-scatter.22
